TPU v7x, 32 devices: a whole 2x2x4 slice. The times are simulated.
32 devices in a mesh: strip: 4 (over z), date: 8 (over y, x, core).
Axes of the slice: x: 2, y: 2, z: 4, core: 2. Of those that a mesh axis runs over, the one named last changes fastest.
Arguments:
- images: bfloat16 [128, 256, 128], P('date', 'strip'), may hold values from 0.19921875 to 5
- inverse_blocks: float32 [2, 8, 128, 128], P(None, 'strip', 'date'), as said below
- pair_first: int32 [256], P('date'), may hold values from 0 to 15
- pair_block: int32 [256, 1], P('date'), may hold values from 0 to 7; in each aligned block of 32 rows (0 to 31, 32 to 63, ...) at most 8 rows name the same one
- pair_second: int32 [256], P('date'), may hold values from 0 to 15
- pair_count: int32 [8], P('date'), may hold values from 8 to 32, as said below
- shifts: int32 [256, 2, 8], P('date', None, 'strip'), may hold values from -8 to 8
- anchors: int32 [8], P('strip'), may hold values from 0 to 96, as said below
Outputs:
- pair_offsets: float32 [256, 2, 8], P('date', None, 'strip')
- series: float32 [2, 8, 128], P(None, 'strip', 'date')
Inputs may be any that keep to these rules, and one draw needn't show every extreme that they name: `pair_block`: among the 32 slots of one date block at most 8 name one partner block, and some block is named that often. `pair_count`: slots 0 to count - 1 of a date block are live; slots at or past the count carry no pair, and their partner windows need not be sent. One block has all 32 live, one has 8, every other block 24 or more. `anchors`: chip q starts at column (q % 2) * 64 plus 0 to 32. `inverse_blocks`: symmetric in its last two dimensions.
All inputs are finite; a program needn't handle non-finite values.
Results may differ from a plain program's by a relative error of at most 0.008.
Values may be sent and summed in bfloat16 or wider, within the bound.
A program may use at most 64 MiB of HBM per device.

v0:
```python
import math
import jax
import jax.numpy as jnp
from jax import lax
from jax.sharding import PartitionSpec as P

SMAX = 8


def padded(cells, sides, width):
    for axis, dim in sides:
        count = lax.axis_size(axis)
        ends = count - 1
        head = lax.slice_in_dim(cells, 0, width, axis=dim)
        tail = lax.slice_in_dim(cells, cells.shape[dim] - width, cells.shape[dim], axis=dim)
        cells = jnp.concatenate(
            [
                lax.ppermute(tail, axis, [(i, (i + 1) % count) for i in range(ends)]),
                cells,
                lax.ppermute(head, axis, [((i + 1) % count, i) for i in range(ends)]),
            ],
            axis=dim,
        )
    return cells


def make_tables(length):
    counter = jnp.arange(length, dtype=jnp.int32)
    products = counter[:, None] * counter[None, :] % length
    radians = products.astype(jnp.float32) * (2.0 * math.pi / length)
    cosine = jnp.cos(radians)
    sine_part = -jnp.sin(radians)
    forward = jnp.concatenate([cosine, sine_part], axis=1).astype(jnp.bfloat16)
    over_len = 2 * length
    signed = jnp.where(counter < length // 2, counter, counter - length)
    places = jnp.arange(over_len, dtype=jnp.int32)
    turned = signed[:, None] * places[None, :] % over_len
    angles = turned.astype(jnp.float32) * (2.0 * math.pi / over_len)
    vcosine = jnp.cos(angles)
    vsine = jnp.sin(angles)
    top_rows = jnp.concatenate([vcosine, vsine], axis=1)
    low_rows = jnp.concatenate([-vsine, vcosine], axis=1)
    inverse_rows = jnp.concatenate([top_rows, low_rows], axis=0).astype(jnp.bfloat16)
    displace = ((places + length) % over_len - length).astype(jnp.float32) * 0.5
    return (
        forward,
        cosine.astype(jnp.bfloat16),
        sine_part.astype(jnp.bfloat16),
        inverse_rows,
        vcosine.T.astype(jnp.bfloat16),
        vsine.T.astype(jnp.bfloat16),
        displace,
    )


def spectra(windows, tables):
    forward, cosine_b, sine_b = (tables[0], tables[1], tables[2])
    length = windows.shape[-1]
    values = windows.astype(jnp.float32)
    centred = (values - jnp.mean(values, axis=(1, 2), keepdims=True)).astype(jnp.bfloat16)
    section_one = jnp.einsum(
        "bmn,nk->bmk", centred, forward, preferred_element_type=jnp.float32
    ).astype(jnp.bfloat16)
    with_cos = jnp.einsum("km,bmj->bkj", cosine_b, section_one, preferred_element_type=jnp.float32)
    with_sin = jnp.einsum("km,bmj->bkj", sine_b, section_one, preferred_element_type=jnp.float32)
    real_part = with_cos[:, :, :length] - with_sin[:, :, length:]
    imag_part = with_sin[:, :, :length] + with_cos[:, :, length:]
    return jnp.concatenate([real_part, imag_part], axis=2).astype(jnp.bfloat16)


def centroid(near_spec, far_spec, tables):
    inverse_rows, back_cos, back_sin, displace = (tables[3], tables[4], tables[5], tables[6])
    length = near_spec.shape[-1] // 2
    near_re = near_spec[:, :, :length].astype(jnp.float32)
    near_im = near_spec[:, :, length:].astype(jnp.float32)
    far_re = far_spec[:, :, :length].astype(jnp.float32)
    far_im = far_spec[:, :, length:].astype(jnp.float32)
    cross_re = near_re * far_re + near_im * far_im
    cross_im = near_im * far_re - near_re * far_im
    cross_spec = jnp.concatenate([cross_re, cross_im], axis=2).astype(jnp.bfloat16)
    along = jnp.einsum(
        "bun,nl->bul", cross_spec, inverse_rows, preferred_element_type=jnp.float32
    ).astype(jnp.bfloat16)
    half_width = along.shape[-1] // 2
    surface = jnp.einsum(
        "ku,bul->bkl", back_cos, along[:, :, :half_width], preferred_element_type=jnp.float32
    )
    surface = surface - jnp.einsum(
        "ku,bul->bkl", back_sin, along[:, :, half_width:], preferred_element_type=jnp.float32
    )
    energy = surface * surface
    norm_val = jnp.mean(energy, axis=(1, 2)) + 1e-06
    row_shift = jnp.mean(energy * displace[None, :, None], axis=(1, 2)) / norm_val
    col_shift = jnp.mean(energy * displace[None, None, :], axis=(1, 2)) / norm_val
    return jnp.stack([row_shift, col_shift], axis=1)


def body(images, inverse_blocks, pair_first, pair_block, pair_second, pair_count, shifts, anchors):
    devices = lax.axis_size("date")
    block_id = lax.axis_index("date")
    dates_dev, length, columns = images.shape
    pair_dev = pair_first.shape[0]
    chip_count = anchors.shape[0]
    capacity = max(2, 2 * pair_dev // devices)
    margin = SMAX
    extent = length + 2 * margin
    tables = make_tables(length)
    target = pair_block[:, 0]
    hit_table = (target[:, None] == jnp.arange(devices, dtype=jnp.int32)[None, :]).astype(jnp.int32)
    earlier = jnp.cumsum(hit_table, axis=0) - hit_table
    rank_in = jnp.sum(earlier * hit_table, axis=1)
    slot_of = target * capacity + rank_in
    requests = (
        jnp.zeros((devices * capacity,), jnp.int32)
        .at[slot_of]
        .set(pair_second)
        .reshape(devices, capacity)
    )
    asked_for = lax.all_to_all(requests, "date", split_axis=0, concat_axis=0, tiled=True)
    wanted = asked_for.reshape(-1)
    picked = jnp.take(images, wanted, axis=0).reshape(devices, capacity, length, columns)
    arrived = lax.all_to_all(picked, "date", split_axis=0, concat_axis=0, tiled=True)
    framed = padded(arrived, (("strip", 2),), margin)
    framed = framed.reshape(devices * capacity, extent, columns)
    framed = jnp.pad(framed, ((0, 0), (0, 0), (margin, margin + length // 2)))
    own_pad = jnp.pad(images, ((0, 0), (0, 0), (0, length // 2)))
    own_list = []
    region_list = []
    for chip_one in range(chip_count):
        own_list.append(lax.dynamic_slice_in_dim(own_pad, anchors[chip_one], length, 2))
        region_list.append(lax.dynamic_slice_in_dim(framed, anchors[chip_one], extent, 2))
    own_windows = jnp.stack(own_list, axis=1)
    regions = jnp.stack(region_list, axis=1)
    own_spec = spectra(own_windows.reshape(-1, length, length), tables).reshape(
        dates_dev, chip_count, length, 2 * length
    )
    step_pairs = math.gcd(pair_dev, max(1, 512 // chip_count))
    turn_count = pair_dev // step_pairs
    inside = jnp.arange(length, dtype=jnp.int32)
    across = jnp.arange(extent, dtype=jnp.int32)

    def one_turn(packed):
        slots_turn, firsts_turn, shifts_turn = packed
        regions_turn = jnp.take(regions, slots_turn, axis=0)
        row_start = margin + shifts_turn[:, 0, :]
        col_start = margin + shifts_turn[:, 1, :]
        row_pick = (
            across[None, None, None, :] == row_start[:, :, None, None] + inside[None, None, :, None]
        ).astype(jnp.bfloat16)
        col_pick = (
            across[None, None, :, None] == col_start[:, :, None, None] + inside[None, None, None, :]
        ).astype(jnp.bfloat16)
        row_cut = jnp.einsum(
            "pcie,pcef->pcif", row_pick, regions_turn, preferred_element_type=jnp.float32
        ).astype(jnp.bfloat16)
        far_windows = jnp.einsum(
            "pcif,pcfj->pcij", row_cut, col_pick, preferred_element_type=jnp.float32
        ).astype(jnp.bfloat16)
        far_spec = spectra(far_windows.reshape(-1, length, length), tables)
        near_spec = jnp.take(own_spec, firsts_turn, axis=0).reshape(-1, length, 2 * length)
        return centroid(near_spec, far_spec, tables).reshape(step_pairs, chip_count, 2)

    packed = (
        slot_of.reshape(turn_count, step_pairs),
        pair_first.reshape(turn_count, step_pairs),
        shifts.reshape(turn_count, step_pairs, 2, chip_count),
    )
    centroids = lax.map(one_turn, packed).reshape(pair_dev, chip_count, 2)
    live_mask = (jnp.arange(pair_dev, dtype=jnp.int32) < pair_count[0]).astype(jnp.float32)
    pair_offsets = (shifts.astype(jnp.float32) + jnp.swapaxes(centroids, 1, 2)) * live_mask[
        :, None, None
    ]
    dates_all = dates_dev * devices
    date_ids = jnp.arange(dates_all, dtype=jnp.int32)
    second_id = target * dates_dev + pair_second
    first_id = block_id * dates_dev + pair_first
    incidence = (second_id[:, None] == date_ids[None, :]).astype(jnp.float32) - (
        first_id[:, None] == date_ids[None, :]
    ).astype(jnp.float32)
    partial_value = jnp.einsum(
        "pxc,pd->xcd", pair_offsets, incidence, precision=lax.Precision.HIGHEST
    )
    rhs_whole = lax.psum(partial_value, "date")
    series = jnp.einsum("xcde,xce->xcd", inverse_blocks, rhs_whole, precision=lax.Precision.HIGHEST)
    return (pair_offsets, series)


def solution(mesh):
    return jax.shard_map(
        body,
        mesh=mesh,
        in_specs=(
            P("date", "strip", None),
            P(None, "strip", "date", None),
            P("date"),
            P("date", None),
            P("date"),
            P("date"),
            P("date", None, "strip"),
            P("strip"),
        ),
        out_specs=(P("date", None, "strip"), P(None, "strip", "date")),
        check_vma=False,
    )
```

profile of v0, /device:TPU:0, one launch (start us, length us, event | category | flops | bytes accessed | tf_op | source)
XLA Modules:
  0.0 84.8 jit_solution(15809964024096351249)
XLA Ops:
  0.6 0.0 copy-start
  0.6 0.7 fusion.76
  1.4 0.1 reduce_window_sum.11
  1.4 0.8 select_reduce_fusion
  2.3 0.7 and_bitcast_fusion
  2.9 0.8 scatter_custom_fusion
  3.7 0.7 all_to_all.9
  4.4 5.2 %all-to-all-start = ((s32[8,1,8]{2,1,0:T(1,128)}), s32[8,1,8]{2,1,0:T(1,128)S(1)}, u32[]{:S(2)}, u32[]{:S(2)}) async-start(s32[8,1,8]{2,1,0:T(1,128)} %bitcast.18), calls=%async_computation | async-start | bytes 8192 | tf_op jit(solution)/shard_map/all_to_all | solution.py:119
  9.6 0.2 negate_convert_fusion.1
  9.8 1.3 %fusion.120 = (s32[1]{0:T(128)}, s32[1]{0:T(128)}) fusion(s32[2]{0:T(128)} %param.15), kind=kLoop, calls=%fused_computation.195 | loop fusion | bytes 16 | tf_op jit(solution)/shard_map/slice | solution.py:131
  15.0 1.3 %fusion.32 = (bf16[16,1,64,64]{3,2,1,0:T(8,128)(2,1)S(1)}, bf16[16,1,64,64]{3,2,1,0:T(8,128)(2,1)S(1)}) fusion(s32[]{:T(128)S(6)} %select_n.129, bf16[16,64,128]{2,1,0:T(8,128)(2,1)} %param.8, s32[]{:T(128)S(6)} %select_n.130), kind=kLoop, calls=%fused_computation.64 | loop fusion | bytes 524296 | tf_op jit(solution)/shard_map/stack | solution.py:132
  16.2 0.1 maximum_convert_fusion
  16.4 0.2 fusion.34
  16.6 0.1 div.58
  16.7 0.2 fusion.26
  16.9 0.0 copy-start.2
  16.9 0.0 copy-start.5
  16.9 0.3 convolution_convert_fusion.2
  17.3 0.4 convolution_bitcast_fusion.2
  17.7 0.4 convolution_bitcast_fusion.3
  18.1 0.1 copy.19
  18.2 0.1 copy.21
  18.3 0.6 fusion.22
  19.0 0.3 pad_maximum_fusion.2
  19.3 0.1 broadcast_in_dim.83
  19.3 0.1 broadcast_in_dim.84
  20.1 0.7 gather_fusion
  20.9 0.6 broadcast.369
  21.5 0.7 reduce.8
  22.2 0.1 reshape.257
  22.3 0.7 gather_fusion.1
  23.1 1.2 %broadcast_select_fusion = bf16[8,8,64,128]{3,2,1,0:T(8,128)(2,1)} fusion(bf16[8,8,64,128]{3,2,1,0:T(8,128)(2,1)S(1)} %bitcast.101, pred[8,8]{1,0:T(8,128)(4,1)S(1)} %compare_and_fusion), kind=kLoop, calls=%fused_computation.58 | loop fusion | flops 524288 | bytes 2097216 | tf_op jit(solution)/shard_map/jit(_take)/select_n | solution.py:121
  24.2 4.2 %all-to-all-start.1 = ((bf16[8,8,64,128]{3,2,1,0:T(8,128)(2,1)}), bf16[8,8,64,128]{3,2,1,0:T(8,128)(2,1)S(1)}, u32[]{:S(2)}, u32[]{:S(2)}) async-start(bf16[8,8,64,128]{3,2,1,0:T(8,128)(2,1)} %broadcast_select_fusion), calls=%async_computation.1 | async-start | bytes 2097152 | tf_op jit(solution)/shard_map/all_to_all | solution.py:122
  28.5 0.2 fusion.75
  28.7 0.1 iota_add_fusion
  28.8 0.2 bitcast_select_fusion
  29.1 14.8 %all-to-all-done.1 = bf16[8,8,64,128]{3,2,1,0:T(8,128)(2,1)S(1)} async-done(((bf16[8,8,64,128]{3,2,1,0:T(8,128)(2,1)}), bf16[8,8,64,128]{3,2,1,0:T(8,128)(2,1)S(1)}, u32[]{:S(2)}, u32[]{:S(2)}) %all-to-all-start.1) | async-done | bytes 1048608 | tf_op jit(solution)/shard_map/all_to_all | solution.py:122
  43.8 0.1 fusion.119
  43.9 3.5 %collective-permute-start = (bf16[8,8,8,128]{3,2,1,0:T(8,128)(2,1)S(1)}, bf16[8,8,8,128]{3,2,1,0:T(8,128)(2,1)S(1)}, u32[]{:S(2)}, u32[]{:S(2)}) collective-permute-start(bf16[8,8,8,128]{3,2,1,0:T(8,128)(2,1)S(1)} %get-tuple-element.68), channel_id=1, source_target_pairs={{0,8},{8,16},{16,24},{1,9},{9,17},{17,25},{2,10},{10,18},{18,26},{... | collective-permute-start | bytes 393224 | tf_op jit(solution)/shard_map/ppermute | solution.py:18
  47.4 1.5 %collective-permute-start.1 = (bf16[8,8,8,128]{3,2,1,0:T(8,128)(2,1)S(1)}, bf16[8,8,8,128]{3,2,1,0:T(8,128)(2,1)S(1)}, u32[]{:S(2)}, u32[]{:S(2)}) collective-permute-start(bf16[8,8,8,128]{3,2,1,0:T(8,128)(2,1)S(1)} %get-tuple-element.69), channel_id=1, source_target_pairs={{8,0},{16,8},{24,16},{9,1},{17,9},{25,17},{10,2},{18,10},{26,18},{... | collective-permute-start | bytes 393224 | tf_op jit(solution)/shard_map/ppermute | solution.py:20
  51.5 2.8 %collective-permute-done.1 = bf16[8,8,8,128]{3,2,1,0:T(8,128)(2,1)S(1)} collective-permute-done((bf16[8,8,8,128]{3,2,1,0:T(8,128)(2,1)S(1)}, bf16[8,8,8,128]{3,2,1,0:T(8,128)(2,1)S(1)}, u32[]{:S(2)}, u32[]{:S(2)}) %collective-permute-start.1) | collective-permute-done | bytes 131104 | tf_op jit(solution)/shard_map/ppermute | solution.py:20
  54.3 0.2 pad_maximum_fusion.1
  54.4 1.1 %fusion.12 = (bf16[64,1,80,80]{3,2,0,1:T(8,128)(2,1)S(1)}, bf16[64,1,80,80]{3,2,0,1:T(8,128)(2,1)S(1)}) fusion(s32[]{:T(128)S(6)} %select_n.137, bf16[64,80,128]{2,1,0:T(8,128)(2,1)S(1)} %bitcast.100, s32[]{:T(128)S(6)} %select_n.138), kind=kLoop, calls=%fused_computation.37 | loop fusion | bytes 2949128 | tf_op jit(solution)/shard_map/stack | solution.py:133
  55.5 2.1 %pad_maximum_fusion = bf16[64,2,80,80]{3,2,0,1:T(8,128)(2,1)} fusion(bf16[64,1,80,80]{3,2,0,1:T(8,128)(2,1)S(1)} %get-tuple-element.67, bf16[64,1,80,80]{3,2,0,1:T(8,128)(2,1)S(1)} %get-tuple-element.66), kind=kLoop, calls=%fused_computation.13 | loop fusion | flops 819200 | bytes 3276800 | tf_op jit(solution)/shard_map/stack | solution.py:133
  57.6 3.5 %gather_fusion.2 = bf16[32,2,80,80]{3,2,1,0:T(8,128)(2,1)} fusion(bf16[64,2,80,80]{3,2,0,1:T(8,128)(2,1)} %pad_maximum_fusion, s32[1024]{0:T(1024)S(1)} %pad_clamp_fusion), kind=kCustom, calls=%fused_computation.2 | custom fusion | bytes 1638528 | tf_op jit(solution)/shard_map/while/body/eval_jaxpr/jit(_take)/gather | solution.py:144
  61.1 2.8 %fusion.121 = (f32[32,2]{1,0:T(8,128)S(1)}, f32[32,2,64,64]{3,2,1,0:T(8,128)S(1)}) fusion(s32[32,2,64]{2,1,0:T(2,128)S(1)} %get-tuple-element.87, bf16[32,2,80,80]{3,2,1,0:T(8,128)(2,1)} %gather_fusion.2, pred[32]{0:T(512)(128)(4,1)S(1)} %get-tuple-element.46, s32[32,2,64]{2,1,0:T(2,128)S(1)} %get-tuple-element.88), kind=kOutput, calls=%fused_computation.196 | convolution fusion | flops 96550848 | bytes 1900832 | tf_op jit(solution)/shard_map/while/body/eval_jaxpr/pcif,pcfj->pcij/dot_general | solution.py:156
  63.9 0.1 div.60
  64.0 0.2 fusion.6
  64.3 0.5 convolution_convert_fusion.1
  64.7 0.5 convolution_bitcast_fusion
  65.3 0.5 convolution_bitcast_fusion.1
  65.8 1.5 %fusion.1 = (bf16[64,64,64]{2,1,0:T(8,128)(2,1)S(1)}, bf16[64,64,64]{2,1,0:T(8,128)(2,1)S(1)}, bf16[64,64,64]{2,1,0:T(8,128)(2,1)S(1)}) fusion(bf16[64,64,128]{2,1,0:T(8,128)(2,1)S(1)} %bitcast_select_fusion, f32[64,64,128]{2,1,0:T(8,128)S(1)} %convolution_bitcast_fusion.1, f32[64,64,128]{2,1,0:T(8,128)S(1)} %convolution_bitcast_fusion), kind=kLoop, calls=%fused_computation.15 | loop fusion | flops 3145728 | bytes 6815744 | tf_op jit(solution)/shard_map/convert.8
  67.3 0.8 fusion.3
  68.1 0.8 convolution_convert_fusion
  68.9 0.9 %fusion.19 = f32[64,128,128]{2,1,0:T(8,128)S(1)} fusion(bf16[64,64,256]{2,1,0:T(8,128)(2,1)S(1)} %convolution_convert_fusion, s32[64]{0:T(128)S(1)} %compare_select_fusion.1), kind=kOutput, calls=%fused_computation.44 | convolution fusion | flops 134340608 | bytes 5243392 | tf_op jit(solution)/shard_map/while/body/eval_jaxpr/ku,bul->bkl/dot_general | solution.py:85
  69.8 1.9 %multiply_reduce_fusion.1 = (f32[64]{0:T(128)S(1)}, f32[64]{0:T(128)S(1)}, f32[64]{0:T(128)S(1)}) fusion(f32[128]{0:T(128)S(1)} %fusion.89, f32[64,128,128]{2,1,0:T(8,128)S(1)} %fusion.19, s32[64]{0:T(128)S(1)} %compare_select_fusion.1, bf16[64,64,256]{2,1,0:T(8,128)(2,1)S(1)} %convolution_convert_fusion), kind=kOutput, calls=%fused_computation.5 | convolution fusion | flops 141680448 | bytes 5245184 | tf_op jit(solution)/shard_map/while/body/eval_jaxpr/ku,bul->bkl/dot_general | solution.py:88
  71.6 0.1 div.64
  71.8 0.1 copy.22
  71.8 0.1 div.67
  71.9 0.1 copy.23
  72.1 0.0 copy-start.4
  72.1 0.2 fusion.63
  72.3 11.8 %psum.7 = f32[2,2,128]{2,1,0:T(2,128)S(1)} all-reduce(f32[2,2,128]{2,1,0:T(2,128)S(1)} %fusion.63), channel_id=1, replica_groups=mesh['strip'=4,'date'=8] {'date'}, use_global_device_ids=true, to_apply=%region_8.9 | all-reduce | flops 512 | bytes 4096 | tf_op jit(solution)/shard_map/psum | solution.py:183
  84.1 0.7 fusion.124
  (29 shorter events, 0.1 us)
Async XLA Ops:
  0.6 83.5 %copy-start = (f32[2,2,16,128]{3,2,1,0:T(8,128)S(1)}, f32[2,2,16,128]{3,2,1,0:T(8,128)}, u32[]{:S(2)}) copy-start(f32[2,2,16,128]{3,2,1,0:T(8,128)} %param.9) | copy-start | bytes 98308
  4.4 16.4 %all-to-all-start = ((s32[8,1,8]{2,1,0:T(1,128)}), s32[8,1,8]{2,1,0:T(1,128)S(1)}, u32[]{:S(2)}, u32[]{:S(2)}) async-start(s32[8,1,8]{2,1,0:T(1,128)} %bitcast.18), calls=%async_computation | async-start | bytes 8192 | tf_op jit(solution)/shard_map/all_to_all | solution.py:119
  16.9 1.2 %copy-start.2 = (s32[32,2,2]{0,2,1:T(2,128)S(1)}, s32[32,2,2]{0,2,1:T(2,128)}, u32[]{:S(2)}) copy-start(s32[32,2,2]{0,2,1:T(2,128)} %param.14) | copy-start | bytes 1540
  16.9 1.4 %copy-start.5 = (s32[32]{0:T(128)S(1)}, s32[32]{0:T(128)}, u32[]{:S(2)}) copy-start(s32[32]{0:T(128)} %param.10) | copy-start | bytes 388
  19.0 3.3 %copy-start.1 = (bf16[16,64,128]{2,1,0:T(8,128)(2,1)S(1)}, bf16[16,64,128]{2,1,0:T(8,128)(2,1)}, u32[]{:S(2)}) copy-start(bf16[16,64,128]{2,1,0:T(8,128)(2,1)} %param.8) | copy-start | bytes 786436
  23.1 5.4 %copy-start.3 = (s32[32,1]{0,1:T(1,128)S(1)}, s32[32,1]{0,1:T(1,128)}, u32[]{:S(2)}) copy-start(s32[32,1]{0,1:T(1,128)} %param.11) | copy-start | bytes 388
  23.1 5.4 %copy-start.6 = (s32[32]{0:T(128)S(1)}, s32[32]{0:T(128)}, u32[]{:S(2)}) copy-start(s32[32]{0:T(128)} %param.12) | copy-start | bytes 388
  24.2 19.6 %all-to-all-start.1 = ((bf16[8,8,64,128]{3,2,1,0:T(8,128)(2,1)}), bf16[8,8,64,128]{3,2,1,0:T(8,128)(2,1)S(1)}, u32[]{:S(2)}, u32[]{:S(2)}) async-start(bf16[8,8,64,128]{3,2,1,0:T(8,128)(2,1)} %broadcast_select_fusion), calls=%async_computation.1 | async-start | bytes 2097152 | tf_op jit(solution)/shard_map/all_to_all | solution.py:122
  43.9 7.6 %collective-permute-start = (bf16[8,8,8,128]{3,2,1,0:T(8,128)(2,1)S(1)}, bf16[8,8,8,128]{3,2,1,0:T(8,128)(2,1)S(1)}, u32[]{:S(2)}, u32[]{:S(2)}) collective-permute-start(bf16[8,8,8,128]{3,2,1,0:T(8,128)(2,1)S(1)} %get-tuple-element.68), channel_id=1, source_target_pairs={{0,8},{8,16},{16,24},{1,9},{9,17},{17,25},{2,10},{10,18},{18,26},{... | collective-permute-start | bytes 393224 | tf_op jit(solution)/shard_map/ppermute | solution.py:18
  47.4 6.9 %collective-permute-start.1 = (bf16[8,8,8,128]{3,2,1,0:T(8,128)(2,1)S(1)}, bf16[8,8,8,128]{3,2,1,0:T(8,128)(2,1)S(1)}, u32[]{:S(2)}, u32[]{:S(2)}) collective-permute-start(bf16[8,8,8,128]{3,2,1,0:T(8,128)(2,1)S(1)} %get-tuple-element.69), channel_id=1, source_target_pairs={{8,0},{16,8},{24,16},{9,1},{17,9},{25,17},{10,2},{18,10},{26,18},{... | collective-permute-start | bytes 393224 | tf_op jit(solution)/shard_map/ppermute | solution.py:20
  72.1 12.8 %copy-start.4 = (f32[32,2,2]{0,2,1:T(2,128)}, f32[32,2,2]{0,2,1:T(2,128)S(1)}, u32[]{:S(2)}) copy-start(f32[32,2,2]{0,2,1:T(2,128)S(1)} %copy.25) | copy-start | bytes 1540
where the time goes:
time: 85.4 us; the launch traced here: 84.8 us
  waiting for transfers between devices  17.5 us (20%)
  starting transfers between devices  14.4 us (17%)
  local copies, waits for them, and re-layouts  11.9 us (14%)
  blocking collectives  11.8 us (14%)
  other arithmetic  11.2 us (13%)
  matrix products  9.92 us (12%)
  between operations  8.17 us (10%)
    all_to_all x1, waiting for transfers between devices, body(): lax.all_to_all(picked, 'date', split_axis=0, concat_axis=0, tiled=True)  14.8 us
    psum x1, blocking collectives, body(): rhs_whole = lax.psum(partial_value, 'date')  11.8 us
    all_to_all x1, starting transfers between devices, body(): lax.all_to_all(requests, 'date', split_axis=0, concat_axis=0, tiled=True)  5.2 us
    all_to_all x1, starting transfers between devices, body(): lax.all_to_all(picked, 'date', split_axis=0, concat_axis=0, tiled=True)  4.2 us
    gather x1, local copies, waits for them, and re-layouts, one_turn(): regions_turn = jnp.take(regions, slots_turn, axis=0)  3.54 us
    ppermute x1, starting transfers between devices, padded(): lax.ppermute(tail, axis, [(i, (i + 1) % count) for i in range(ends)])  3.49 us
    another operation x5, other arithmetic  3.26 us
    ppermute x1, waiting for transfers between devices, padded(): lax.ppermute(head, axis, [((i + 1) % count, i) for i in range(ends)])  2.76 us
  transfers between devices with their start and end apart: 4, of which 2 were waited for; matrix products, arithmetic and copies ran while one was open for 8% of the time, Pallas kernels for 0%

commit v1 on v0

--- a/solution.py
+++ b/solution.py
@@ -180,7 +180,7 @@
     partial_value = jnp.einsum(
         "pxc,pd->xcd", pair_offsets, incidence, precision=lax.Precision.HIGHEST
     )
-    rhs_whole = lax.psum(partial_value, "date")
+    rhs_whole = jnp.sum(lax.all_gather(partial_value, "date"), axis=0)
     series = jnp.einsum("xcde,xce->xcd", inverse_blocks, rhs_whole, precision=lax.Precision.HIGHEST)
     return (pair_offsets, series)
 

time: 85.4 us -> 81.8 us (0.958)
  blocking collectives: 11.8 us -> 8.14 us
    psum x1 -> x0, blocking collectives: 11.8 us -> none  [body(): rhs_whole = lax.psum(partial_value, 'date')]
    all_gather x0 -> x1, blocking collectives: none -> 8.14 us  [body(): rhs_whole = jnp.sum(lax.all_gather(partial_value, 'date'), axis=0)]
  transfers between devices with their start and end apart: 4 -> 4, of which waited for: 2 -> 2; matrix products, arithmetic and copies ran while one was open for 8% -> 9% of each run, Pallas kernels for 0% -> 0%
where the time goes in v1:
time: 81.8 us; the launch traced here: 81.2 us
  waiting for transfers between devices  17.5 us (21%)
  starting transfers between devices  14.4 us (18%)
  local copies, waits for them, and re-layouts  11.9 us (15%)
  other arithmetic  11.2 us (14%)
  matrix products  9.92 us (12%)
  between operations  8.18 us (10%)
  blocking collectives  8.14 us (10%)
    all_to_all x1, waiting for transfers between devices, body(): lax.all_to_all(picked, 'date', split_axis=0, concat_axis=0, tiled=True)  14.8 us
    all_gather x1, blocking collectives, body(): rhs_whole = jnp.sum(lax.all_gather(partial_value, 'date'), axis=0)  8.14 us
    all_to_all x1, starting transfers between devices, body(): lax.all_to_all(requests, 'date', split_axis=0, concat_axis=0, tiled=True)  5.2 us
    all_to_all x1, starting transfers between devices, body(): lax.all_to_all(picked, 'date', split_axis=0, concat_axis=0, tiled=True)  4.2 us
    gather x1, local copies, waits for them, and re-layouts, one_turn(): regions_turn = jnp.take(regions, slots_turn, axis=0)  3.54 us
    ppermute x1, starting transfers between devices, padded(): lax.ppermute(tail, axis, [(i, (i + 1) % count) for i in range(ends)])  3.49 us
    another operation x5, other arithmetic  3.26 us
    ppermute x1, waiting for transfers between devices, padded(): lax.ppermute(head, axis, [((i + 1) % count, i) for i in range(ends)])  2.76 us
  transfers between devices with their start and end apart: 4, of which 2 were waited for; matrix products, arithmetic and copies ran while one was open for 9% of the time, Pallas kernels for 0%

profile of v1, /device:TPU:0, one launch (start us, length us, event | category | flops | bytes accessed | tf_op | source)
XLA Modules:
  0.0 81.2 jit_solution(1901929643984415560)
XLA Ops:
  0.6 0.0 copy-start
  0.6 0.7 fusion.76
  1.4 0.1 reduce_window_sum.11
  1.4 0.8 %select_reduce_fusion = s32[32]{0:T(128)S(1)} fusion(s32[32,8]{1,0:T(8,128)S(1)} %reduce_window_sum.11, s32[32]{0:T(128)} %bitcast.109), kind=kLoop, calls=%fused_computation.125 | loop fusion | flops 1248 | bytes 1280 | tf_op jit(solution)/shard_map/reduce_sum | solution.py:111
  2.3 0.7 and_bitcast_fusion
  2.9 0.8 scatter_custom_fusion
  3.7 0.7 all_to_all.9
  4.4 5.2 %all-to-all-start = ((s32[8,1,8]{2,1,0:T(1,128)}), s32[8,1,8]{2,1,0:T(1,128)S(1)}, u32[]{:S(2)}, u32[]{:S(2)}) async-start(s32[8,1,8]{2,1,0:T(1,128)} %bitcast.18), calls=%async_computation | async-start | bytes 8192 | tf_op jit(solution)/shard_map/all_to_all | solution.py:119
  9.6 0.2 negate_convert_fusion.1
  9.8 1.3 %fusion.120 = (s32[1]{0:T(128)}, s32[1]{0:T(128)}) fusion(s32[2]{0:T(128)} %param.15), kind=kLoop, calls=%fused_computation.195 | loop fusion | bytes 16 | tf_op jit(solution)/shard_map/slice | solution.py:131
  15.0 1.3 %fusion.32 = (bf16[16,1,64,64]{3,2,1,0:T(8,128)(2,1)S(1)}, bf16[16,1,64,64]{3,2,1,0:T(8,128)(2,1)S(1)}) fusion(s32[]{:T(128)S(6)} %select_n.129, bf16[16,64,128]{2,1,0:T(8,128)(2,1)} %param.8, s32[]{:T(128)S(6)} %select_n.130), kind=kLoop, calls=%fused_computation.64 | loop fusion | bytes 524296 | tf_op jit(solution)/shard_map/stack | solution.py:132
  16.2 0.1 maximum_convert_fusion
  16.4 0.2 fusion.34
  16.6 0.1 div.58
  16.7 0.2 fusion.26
  16.9 0.0 copy-start.2
  16.9 0.0 copy-start.5
  16.9 0.3 convolution_convert_fusion.2
  17.3 0.4 convolution_bitcast_fusion.2
  17.7 0.4 convolution_bitcast_fusion.3
  18.1 0.1 copy.21
  18.2 0.1 copy.23
  18.3 0.6 fusion.22
  19.0 0.3 pad_maximum_fusion.2
  19.3 0.1 broadcast_in_dim.83
  19.3 0.1 broadcast_in_dim.84
  20.1 0.7 gather_fusion
  20.9 0.6 broadcast.369
  21.5 0.7 reduce.8
  22.2 0.1 reshape.257
  22.3 0.7 gather_fusion.1
  23.1 1.2 %broadcast_select_fusion = bf16[8,8,64,128]{3,2,1,0:T(8,128)(2,1)} fusion(bf16[8,8,64,128]{3,2,1,0:T(8,128)(2,1)S(1)} %bitcast.102, pred[8,8]{1,0:T(8,128)(4,1)S(1)} %compare_and_fusion), kind=kLoop, calls=%fused_computation.58 | loop fusion | flops 524288 | bytes 2097216 | tf_op jit(solution)/shard_map/jit(_take)/select_n | solution.py:121
  24.2 4.2 %all-to-all-start.1 = ((bf16[8,8,64,128]{3,2,1,0:T(8,128)(2,1)}), bf16[8,8,64,128]{3,2,1,0:T(8,128)(2,1)S(1)}, u32[]{:S(2)}, u32[]{:S(2)}) async-start(bf16[8,8,64,128]{3,2,1,0:T(8,128)(2,1)} %broadcast_select_fusion), calls=%async_computation.1 | async-start | bytes 2097152 | tf_op jit(solution)/shard_map/all_to_all | solution.py:122
  28.5 0.2 fusion.75
  28.7 0.1 iota_add_fusion
  28.8 0.2 bitcast_select_fusion
  29.1 14.8 %all-to-all-done.1 = bf16[8,8,64,128]{3,2,1,0:T(8,128)(2,1)S(1)} async-done(((bf16[8,8,64,128]{3,2,1,0:T(8,128)(2,1)}), bf16[8,8,64,128]{3,2,1,0:T(8,128)(2,1)S(1)}, u32[]{:S(2)}, u32[]{:S(2)}) %all-to-all-start.1) | async-done | bytes 1048608 | tf_op jit(solution)/shard_map/all_to_all | solution.py:122
  43.8 0.1 fusion.119
  43.9 3.5 %collective-permute-start = (bf16[8,8,8,128]{3,2,1,0:T(8,128)(2,1)S(1)}, bf16[8,8,8,128]{3,2,1,0:T(8,128)(2,1)S(1)}, u32[]{:S(2)}, u32[]{:S(2)}) collective-permute-start(bf16[8,8,8,128]{3,2,1,0:T(8,128)(2,1)S(1)} %get-tuple-element.68), channel_id=1, source_target_pairs={{0,8},{8,16},{16,24},{1,9},{9,17},{17,25},{2,10},{10,18},{18,26},{... | collective-permute-start | bytes 393224 | tf_op jit(solution)/shard_map/ppermute | solution.py:18
  47.4 1.5 %collective-permute-start.1 = (bf16[8,8,8,128]{3,2,1,0:T(8,128)(2,1)S(1)}, bf16[8,8,8,128]{3,2,1,0:T(8,128)(2,1)S(1)}, u32[]{:S(2)}, u32[]{:S(2)}) collective-permute-start(bf16[8,8,8,128]{3,2,1,0:T(8,128)(2,1)S(1)} %get-tuple-element.69), channel_id=1, source_target_pairs={{8,0},{16,8},{24,16},{9,1},{17,9},{25,17},{10,2},{18,10},{26,18},{... | collective-permute-start | bytes 393224 | tf_op jit(solution)/shard_map/ppermute | solution.py:20
  51.5 2.8 %collective-permute-done.1 = bf16[8,8,8,128]{3,2,1,0:T(8,128)(2,1)S(1)} collective-permute-done((bf16[8,8,8,128]{3,2,1,0:T(8,128)(2,1)S(1)}, bf16[8,8,8,128]{3,2,1,0:T(8,128)(2,1)S(1)}, u32[]{:S(2)}, u32[]{:S(2)}) %collective-permute-start.1) | collective-permute-done | bytes 131104 | tf_op jit(solution)/shard_map/ppermute | solution.py:20
  54.3 0.2 pad_maximum_fusion.1
  54.4 1.1 %fusion.12 = (bf16[64,1,80,80]{3,2,0,1:T(8,128)(2,1)S(1)}, bf16[64,1,80,80]{3,2,0,1:T(8,128)(2,1)S(1)}) fusion(s32[]{:T(128)S(6)} %select_n.137, bf16[64,80,128]{2,1,0:T(8,128)(2,1)S(1)} %bitcast.101, s32[]{:T(128)S(6)} %select_n.138), kind=kLoop, calls=%fused_computation.37 | loop fusion | bytes 2949128 | tf_op jit(solution)/shard_map/stack | solution.py:133
  55.5 2.1 %pad_maximum_fusion = bf16[64,2,80,80]{3,2,0,1:T(8,128)(2,1)} fusion(bf16[64,1,80,80]{3,2,0,1:T(8,128)(2,1)S(1)} %get-tuple-element.67, bf16[64,1,80,80]{3,2,0,1:T(8,128)(2,1)S(1)} %get-tuple-element.66), kind=kLoop, calls=%fused_computation.13 | loop fusion | flops 819200 | bytes 3276800 | tf_op jit(solution)/shard_map/stack | solution.py:133
  57.6 3.5 %gather_fusion.2 = bf16[32,2,80,80]{3,2,1,0:T(8,128)(2,1)} fusion(bf16[64,2,80,80]{3,2,0,1:T(8,128)(2,1)} %pad_maximum_fusion, s32[1024]{0:T(1024)S(1)} %pad_clamp_fusion), kind=kCustom, calls=%fused_computation.2 | custom fusion | bytes 1638528 | tf_op jit(solution)/shard_map/while/body/eval_jaxpr/jit(_take)/gather | solution.py:144
  61.1 2.8 %fusion.121 = (f32[32,2]{1,0:T(8,128)S(1)}, f32[32,2,64,64]{3,2,1,0:T(8,128)S(1)}) fusion(s32[32,2,64]{2,1,0:T(2,128)S(1)} %get-tuple-element.87, bf16[32,2,80,80]{3,2,1,0:T(8,128)(2,1)} %gather_fusion.2, pred[32]{0:T(512)(128)(4,1)S(1)} %get-tuple-element.46, s32[32,2,64]{2,1,0:T(2,128)S(1)} %get-tuple-element.88), kind=kOutput, calls=%fused_computation.196 | convolution fusion | flops 96550848 | bytes 1900832 | tf_op jit(solution)/shard_map/while/body/eval_jaxpr/pcif,pcfj->pcij/dot_general | solution.py:156
  63.9 0.1 div.60
  64.0 0.2 fusion.6
  64.3 0.5 convolution_convert_fusion.1
  64.7 0.5 convolution_bitcast_fusion
  65.3 0.5 convolution_bitcast_fusion.1
  65.8 1.5 %fusion.1 = (bf16[64,64,64]{2,1,0:T(8,128)(2,1)S(1)}, bf16[64,64,64]{2,1,0:T(8,128)(2,1)S(1)}, bf16[64,64,64]{2,1,0:T(8,128)(2,1)S(1)}) fusion(bf16[64,64,128]{2,1,0:T(8,128)(2,1)S(1)} %bitcast_select_fusion, f32[64,64,128]{2,1,0:T(8,128)S(1)} %convolution_bitcast_fusion.1, f32[64,64,128]{2,1,0:T(8,128)S(1)} %convolution_bitcast_fusion), kind=kLoop, calls=%fused_computation.15 | loop fusion | flops 3145728 | bytes 6815744 | tf_op jit(solution)/shard_map/convert.8
  67.3 0.8 fusion.3
  68.1 0.8 convolution_convert_fusion
  68.9 0.9 %fusion.19 = f32[64,128,128]{2,1,0:T(8,128)S(1)} fusion(bf16[64,64,256]{2,1,0:T(8,128)(2,1)S(1)} %convolution_convert_fusion, s32[64]{0:T(128)S(1)} %compare_select_fusion.1), kind=kOutput, calls=%fused_computation.44 | convolution fusion | flops 134340608 | bytes 5243392 | tf_op jit(solution)/shard_map/while/body/eval_jaxpr/ku,bul->bkl/dot_general | solution.py:85
  69.8 1.9 %multiply_reduce_fusion.1 = (f32[64]{0:T(128)S(1)}, f32[64]{0:T(128)S(1)}, f32[64]{0:T(128)S(1)}) fusion(f32[128]{0:T(128)S(1)} %fusion.89, f32[64,128,128]{2,1,0:T(8,128)S(1)} %fusion.19, s32[64]{0:T(128)S(1)} %compare_select_fusion.1, bf16[64,64,256]{2,1,0:T(8,128)(2,1)S(1)} %convolution_convert_fusion), kind=kOutput, calls=%fused_computation.5 | convolution fusion | flops 141680448 | bytes 5245184 | tf_op jit(solution)/shard_map/while/body/eval_jaxpr/ku,bul->bkl/dot_general | solution.py:88
  71.6 0.1 div.64
  71.8 0.1 copy.24
  71.8 0.1 div.67
  71.9 0.1 copy.25
  72.1 0.0 copy-start.4
  72.1 0.2 fusion.63
  72.3 8.1 %all-gather = f32[16,2,128]{2,1,0:T(2,128)S(1)} all-gather(f32[2,2,128]{2,1,0:T(2,128)S(1)} %fusion.63), channel_id=2, replica_groups=mesh['strip'=4,'date'=8] {'date'}, dimensions={0}, use_global_device_ids=true | all-gather | bytes 18432 | tf_op jit(solution)/shard_map/all_gather | solution.py:183
  80.5 0.7 fusion.124
  (30 shorter events, 0.2 us)
Async XLA Ops:
  0.6 79.8 %copy-start = (f32[2,2,16,128]{3,2,1,0:T(8,128)S(1)}, f32[2,2,16,128]{3,2,1,0:T(8,128)}, u32[]{:S(2)}) copy-start(f32[2,2,16,128]{3,2,1,0:T(8,128)} %param.9) | copy-start | bytes 98308
  4.4 16.4 %all-to-all-start = ((s32[8,1,8]{2,1,0:T(1,128)}), s32[8,1,8]{2,1,0:T(1,128)S(1)}, u32[]{:S(2)}, u32[]{:S(2)}) async-start(s32[8,1,8]{2,1,0:T(1,128)} %bitcast.18), calls=%async_computation | async-start | bytes 8192 | tf_op jit(solution)/shard_map/all_to_all | solution.py:119
  16.9 1.2 %copy-start.2 = (s32[32,2,2]{0,2,1:T(2,128)S(1)}, s32[32,2,2]{0,2,1:T(2,128)}, u32[]{:S(2)}) copy-start(s32[32,2,2]{0,2,1:T(2,128)} %param.14) | copy-start | bytes 1540
  16.9 1.4 %copy-start.5 = (s32[32]{0:T(128)S(1)}, s32[32]{0:T(128)}, u32[]{:S(2)}) copy-start(s32[32]{0:T(128)} %param.10) | copy-start | bytes 388
  19.0 3.3 %copy-start.1 = (bf16[16,64,128]{2,1,0:T(8,128)(2,1)S(1)}, bf16[16,64,128]{2,1,0:T(8,128)(2,1)}, u32[]{:S(2)}) copy-start(bf16[16,64,128]{2,1,0:T(8,128)(2,1)} %param.8) | copy-start | bytes 786436
  23.1 5.4 %copy-start.3 = (s32[32,1]{0,1:T(1,128)S(1)}, s32[32,1]{0,1:T(1,128)}, u32[]{:S(2)}) copy-start(s32[32,1]{0,1:T(1,128)} %param.11) | copy-start | bytes 388
  23.1 5.4 %copy-start.6 = (s32[32]{0:T(128)S(1)}, s32[32]{0:T(128)}, u32[]{:S(2)}) copy-start(s32[32]{0:T(128)} %param.12) | copy-start | bytes 388
  24.2 19.6 %all-to-all-start.1 = ((bf16[8,8,64,128]{3,2,1,0:T(8,128)(2,1)}), bf16[8,8,64,128]{3,2,1,0:T(8,128)(2,1)S(1)}, u32[]{:S(2)}, u32[]{:S(2)}) async-start(bf16[8,8,64,128]{3,2,1,0:T(8,128)(2,1)} %broadcast_select_fusion), calls=%async_computation.1 | async-start | bytes 2097152 | tf_op jit(solution)/shard_map/all_to_all | solution.py:122
  43.9 7.6 %collective-permute-start = (bf16[8,8,8,128]{3,2,1,0:T(8,128)(2,1)S(1)}, bf16[8,8,8,128]{3,2,1,0:T(8,128)(2,1)S(1)}, u32[]{:S(2)}, u32[]{:S(2)}) collective-permute-start(bf16[8,8,8,128]{3,2,1,0:T(8,128)(2,1)S(1)} %get-tuple-element.68), channel_id=1, source_target_pairs={{0,8},{8,16},{16,24},{1,9},{9,17},{17,25},{2,10},{10,18},{18,26},{... | collective-permute-start | bytes 393224 | tf_op jit(solution)/shard_map/ppermute | solution.py:18
  47.4 6.9 %collective-permute-start.1 = (bf16[8,8,8,128]{3,2,1,0:T(8,128)(2,1)S(1)}, bf16[8,8,8,128]{3,2,1,0:T(8,128)(2,1)S(1)}, u32[]{:S(2)}, u32[]{:S(2)}) collective-permute-start(bf16[8,8,8,128]{3,2,1,0:T(8,128)(2,1)S(1)} %get-tuple-element.69), channel_id=1, source_target_pairs={{8,0},{16,8},{24,16},{9,1},{17,9},{25,17},{10,2},{18,10},{26,18},{... | collective-permute-start | bytes 393224 | tf_op jit(solution)/shard_map/ppermute | solution.py:20
  72.1 9.2 %copy-start.4 = (f32[32,2,2]{0,2,1:T(2,128)}, f32[32,2,2]{0,2,1:T(2,128)S(1)}, u32[]{:S(2)}) copy-start(f32[32,2,2]{0,2,1:T(2,128)S(1)} %copy.27) | copy-start | bytes 1540
